TPU v7x, 256 devices: a whole 4x4x8 slice. The times are simulated.
256 devices in a mesh: state: 8 (over z), tile: 32 (over x, y, core).
Axes of the slice: x: 4, y: 4, z: 8, core: 2. Of those that a mesh axis runs over, the one named last changes fastest.
Arguments:
- bands: bfloat16 [8, 240, 524288], P('state', None, 'tile')
- block_slot: int32 [8, 4096], P('state', 'tile'), may hold values from 0 to 7
- tile_counties: int32 [8, 256], P('state', 'tile'), may hold values from 0 to 383, as said below
- county_place: int32 [8, 384], P('state'), may hold values from 0 to 383, as said below
- label: int32 [8, 384], P('state', 'tile'), may hold values from -200 to 200
- w_first: bfloat16 [64, 240], replicated, may hold values from -0.375 to 0.375
- taps: float32 [3, 64], replicated, may hold values from -2 to 2
- w_second: bfloat16 [128, 64], replicated, may hold values from -0.75 to 0.75
- w_third: bfloat16 [128, 128], replicated, may hold values from -0.5 to 0.5
- w_head: bfloat16 [128], replicated, may hold values from -0.5 to 0.5
Outputs:
- county_mean: float32 [8, 384], P('state', 'tile')
- weight_grads: float32 [40256], replicated
Inputs may be any that keep to these rules, and one draw needn't show every extreme that they name: `county_place`: each row is an ordering of the counties of one state region; the county at place p is owned by tile index p // 12 of that region. `tile_counties`: tile t's list names counties of its own state region owned by tile indices t, t + 1, ..., t + 4 - 1 (mod the tile axis's size); at most 4 entries of a list are owned by one tile index, and exactly 4 by t itself.
All inputs are finite; a program needn't handle non-finite values.
Results may differ from a plain program's by a relative error of at most 0.00064.
Values sent between devices are 32-bit elements; how exact they have to be, the bound alone decides.
No kernel may reach another device: no remote copies, remote signals or barrier semaphores. Data moves between devices by JAX's collectives and lax.ppermute only.
A program may use at most 128 MiB of HBM per device.

v0:
```python
import jax
import jax.numpy as jnp
from jax import lax
from jax.sharding import PartitionSpec as P

MOST = 4
REACH = 4


def from_behind(value, axis, by):
    peers = lax.axis_size(axis)
    return lax.ppermute(value, axis, [(i, (i + by) % peers) for i in range(peers)])


def silu_parts(value):
    sig = jax.nn.sigmoid(value)
    return (value * sig, sig * (1.0 + value * (1.0 - sig)))


def along_rows(field, weights, row_len):
    chans, count = field.shape
    grid = field.reshape(chans, count // row_len, row_len)
    padded = jnp.pad(grid, ((0, 0), (0, 0), (1, 1)))
    out = (
        weights[0][:, None, None] * padded[:, :, :-2]
        + weights[1][:, None, None] * grid
        + weights[2][:, None, None] * padded[:, :, 2:]
    )
    return out.reshape(chans, count)


def tap_grads(field, upstream, row_len):
    chans, count = field.shape
    grid = field.reshape(chans, count // row_len, row_len)
    padded = jnp.pad(grid, ((0, 0), (0, 0), (1, 1)))
    above = upstream.reshape(grid.shape)
    return jnp.stack(
        [
            jnp.sum(above * padded[:, :, :-2], axis=(1, 2)),
            jnp.sum(above * grid, axis=(1, 2)),
            jnp.sum(above * padded[:, :, 2:], axis=(1, 2)),
        ]
    )


def contract_last(left, right):
    return lax.dot_general(
        left, right, (((1,), (1,)), ((), ())), preferred_element_type=jnp.float32
    )


def contract_first(left, right):
    return lax.dot_general(
        left, right, (((0,), (0,)), ((), ())), preferred_element_type=jnp.float32
    )


def forward(pixels, w_first, taps, w_second, w_third, w_head, row_len):
    h_one = jnp.dot(w_first, pixels, preferred_element_type=jnp.float32)
    s_one = along_rows(h_one, taps, row_len)
    a_one = silu_parts(s_one)[0].astype(jnp.bfloat16)
    h_two = jnp.dot(w_second, a_one, preferred_element_type=jnp.float32)
    a_two = silu_parts(h_two)[0].astype(jnp.bfloat16)
    h_three = jnp.dot(w_third, a_two, preferred_element_type=jnp.float32)
    a_three = (silu_parts(h_three)[0] + a_two.astype(jnp.float32)).astype(jnp.bfloat16)
    yhat = jnp.dot(w_head, a_three, preferred_element_type=jnp.float32)
    return (h_one, s_one, a_one, h_two, a_two, h_three, a_three, yhat)


def backward(pixels, saved, taps, w_second, w_third, w_head, cotangent, row_len):
    h_one, s_one, a_one, h_two, a_two, h_three, a_three, yhat = saved
    grad_in = cotangent.astype(jnp.bfloat16)
    d_head = jnp.dot(a_three, grad_in, preferred_element_type=jnp.float32)
    d_a3 = w_head.astype(jnp.float32)[:, None] * grad_in.astype(jnp.float32)[None, :]
    d_h3 = (d_a3 * silu_parts(h_three)[1]).astype(jnp.bfloat16)
    d_third = contract_last(d_h3, a_two)
    d_a2 = contract_first(w_third, d_h3) + d_a3
    d_h2 = (d_a2 * silu_parts(h_two)[1]).astype(jnp.bfloat16)
    d_second = contract_last(d_h2, a_one)
    d_a1 = contract_first(w_second, d_h2)
    d_s1 = d_a1 * silu_parts(s_one)[1]
    d_taps = tap_grads(h_one, d_s1, row_len)
    d_h1 = along_rows(d_s1, jnp.stack([taps[2], taps[1], taps[0]]), row_len).astype(jnp.bfloat16)
    d_first = contract_last(d_h1, pixels)
    return jnp.concatenate(
        [d_first.reshape(-1), d_taps.reshape(-1), d_second.reshape(-1), d_third.reshape(-1), d_head]
    )


def slot_stats(yhat, slots, slot_count):
    blocks = slots.shape[0]
    row_len = yhat.shape[0] // blocks
    member = (slots[None, :] == jnp.arange(slot_count, dtype=jnp.int32)[:, None]).astype(
        jnp.float32
    )
    block_sums = jnp.sum(yhat.reshape(blocks, row_len), axis=1)
    return (
        jnp.sum(member * block_sums[None, :], axis=1),
        jnp.sum(member, axis=1) * row_len,
        member,
    )


def place_of(counties, table):
    hits = counties[:, None] == jnp.arange(table.shape[0], dtype=jnp.int32)[None, :]
    return jnp.sum(jnp.where(hits, table[None, :], 0), axis=1)


def judge(sums, counts, labels, devices):
    denom = jnp.maximum(counts, 1.0)
    mean = sums / denom
    live = (counts > 0.5).astype(jnp.float32)
    target = labels.astype(jnp.float32) * 0.01
    return (mean, live * 2.0 * (mean - target) / (devices * denom))


def pixel_cotangent(member, slot_adjoint, row_len):
    block_adjoint = jnp.sum(member * slot_adjoint[:, None], axis=0)
    return jnp.broadcast_to(block_adjoint[:, None], (block_adjoint.shape[0], row_len)).reshape(-1)


def settle(sums, counts, codes, labels, devices):
    flat_codes = codes.reshape(-1)
    owned = jnp.arange(1, labels.shape[0] + 1, dtype=jnp.int32).astype(jnp.float32)
    hit = (flat_codes[:, None] == owned[None, :]).astype(jnp.float32)
    total = jnp.sum(hit * sums.reshape(-1)[:, None], axis=0)
    number = jnp.sum(hit * counts.reshape(-1)[:, None], axis=0)
    mean, adjoint = judge(total, number, labels, devices)
    back = jnp.sum(hit * adjoint[None, :], axis=1).reshape(codes.shape)
    return (mean, back)


def packed(select, values, rows):
    return jnp.sum(select * values[:, None], axis=0).reshape(rows, -1)


def on_device(
    bands, block_slot, tile_counties, county_place, label, w_first, taps, w_second, w_third, w_head
):
    pixels = bands[0]
    slots = block_slot[0]
    row_len = pixels.shape[1] // slots.shape[0]
    slot_total = tile_counties.shape[1]
    saved = forward(pixels, w_first, taps, w_second, w_third, w_head, row_len)
    slot_sums, slot_counts, member = slot_stats(saved[-1], slots, slot_total)
    table = county_place[0]
    place = place_of(tile_counties[0], table)
    labels_mine = label[0]
    cty_dev = labels_mine.shape[0]
    n_tile = lax.axis_size("tile")
    devices = float(lax.axis_size("state") * n_tile)
    owner = place // cty_dev
    local_code = (place % cty_dev + 1).astype(jnp.float32)
    order = jnp.arange(slot_total, dtype=jnp.int32)
    rank = jnp.sum(
        ((owner[:, None] == owner[None, :]) & (order[None, :] < order[:, None])).astype(jnp.int32),
        axis=1,
    )
    me = lax.axis_index("tile")
    position = (owner - me) % n_tile * MOST + rank
    select = (position[:, None] == jnp.arange(REACH * MOST, dtype=jnp.int32)[None, :]).astype(
        jnp.float32
    )
    out_sums = packed(select, slot_sums, REACH)
    out_counts = packed(select, slot_counts, REACH)
    out_codes = packed(select, local_code, REACH)
    got_sums, got_counts, got_codes = ([], [], [])
    for step in range(REACH):
        if step == 0:
            piece = (out_sums[0], out_counts[0], out_codes[0])
        else:
            piece = from_behind((out_sums[step], out_counts[step], out_codes[step]), "tile", step)
        got_sums.append(piece[0])
        got_counts.append(piece[1])
        got_codes.append(piece[2])
    county_mean, back = settle(
        jnp.stack(got_sums), jnp.stack(got_counts), jnp.stack(got_codes), labels_mine, devices
    )
    rows = []
    for step in range(REACH):
        if step == 0:
            rows.append(back[0])
        else:
            rows.append(from_behind(back[step], "tile", -step))
    returned = jnp.stack(rows).reshape(-1)
    slot_adjoint = jnp.sum(select * returned[None, :], axis=1)
    cotangent = pixel_cotangent(member, slot_adjoint, row_len)
    local_grads = backward(pixels, saved, taps, w_second, w_third, w_head, cotangent, row_len)
    weight_grads = lax.psum(local_grads, ("state", "tile"))
    return (county_mean[None, :], weight_grads)


def solution(mesh):
    in_specs = (
        P("state", None, "tile"),
        P("state", "tile"),
        P("state", "tile"),
        P("state", None),
        P("state", "tile"),
        P(),
        P(),
        P(),
        P(),
        P(),
    )
    out_specs = (P("state", "tile"), P())
    return jax.shard_map(
        on_device, mesh=mesh, in_specs=in_specs, out_specs=out_specs, check_vma=False
    )
```

profile of v0, /device:TPU:1, one launch (start us, length us, event | category | flops | bytes accessed | tf_op | source)
XLA Modules:
  0.0 352.5 jit_solution(9751502985637400692)
XLA Ops:
  7.2 0.8 slice_bitcast_fusion.5
  8.0 4.7 %fusion.5 = f32[64,128,128]{2,0,1:T(8,128)S(1)} fusion(bf16[64,240]{1,0:T(8,128)(2,1)} %param.15, bf16[1,240,16384]{2,1,0:T(8,128)(2,1)} %param.10), kind=kOutput, calls=%fused_computation.18 | convolution fusion | flops 503316480 | bytes 12089344 | tf_op jit(solution)/shard_map/dot_general | solution.py:59
  12.8 2.4 fusion.18
  15.2 4.6 %multiply_convert_fusion = (bf16[128,16384]{0,1:T(8,128)(2,1)S(1)}, f32[128,16384]{0,1:T(8,128)}) fusion(bf16[64,16384]{1,0:T(8,128)(2,1)S(1)} %fusion.18, bf16[128,64]{0,1:T(8,128)(2,1)S(1)} %copy-done.12), kind=kOutput, calls=%fused_computation.16 | convolution fusion | flops 278921216 | bytes 14696448 | tf_op jit(solution)/shard_map/dot_general | solution.py:62
  19.8 4.6 %add_convert_fusion = (bf16[128,16384]{0,1:T(8,128)(2,1)S(1)}, f32[128,16384]{0,1:T(8,128)}) fusion(bf16[128,16384]{0,1:T(8,128)(2,1)S(1)} %get-tuple-element.37, bf16[128,128]{1,0:T(8,128)(2,1)S(1)} %copy-done), kind=kOutput, calls=%fused_computation.14 | convolution fusion | flops 551550976 | bytes 16809984 | tf_op jit(solution)/shard_map/dot_general | solution.py:64
  24.5 1.9 copy-done.3
  26.5 1.2 fusion.38
  27.6 0.1 reduce_sum.147
  27.8 0.1 convert_reduce_fusion
  28.0 0.2 select_reduce_fusion
  28.2 0.2 convert_reduce_fusion.1
  28.5 2.7 collective-permute-start.3
  31.2 1.3 collective-permute-start.4
  32.5 1.7 collective-permute-start.5
  34.3 0.5 collective-permute-start
  34.7 1.3 collective-permute-start.1
  36.1 2.1 collective-permute-start.2
  38.3 0.5 collective-permute-start.6
  38.7 0.1 collective-permute-done.5
  38.8 0.8 collective-permute-start.7
  39.7 2.2 collective-permute-start.8
  41.9 0.6 collective-permute-done.2
  42.6 2.0 collective-permute-done.7
  44.6 1.5 collective-permute-done.8
  46.1 0.1 fusion.27
  46.2 0.5 fusion.40
  46.8 0.2 fusion.28
  47.0 0.9 collective-permute-start.9
  47.9 2.0 collective-permute-start.10
  49.9 0.3 collective-permute-start.11
  50.2 0.4 collective-permute-done.10
  50.6 3.8 %collective-permute-done.11 = f32[4]{0:T(128)S(1)} collective-permute-done((f32[4]{0:T(128)S(1)}, f32[4]{0:T(128)S(1)}, u32[]{:S(2)}, u32[]{:S(2)}) %collective-permute-start.11) | collective-permute-done | bytes 48 | tf_op jit(solution)/shard_map/ppermute | solution.py:12
  54.5 0.2 select_reduce_fusion.2
  54.9 10.0 %fusion.4 = bf16[128,16384]{0,1:T(8,128)(2,1)S(1)} fusion(f32[128,16384]{0,1:T(8,128)} %get-tuple-element.40, f32[16384]{0:T(1024)S(1)} %get-tuple-element.18, f32[128]{0:T(128)S(1)} %convert_element_type.84), kind=kLoop, calls=%fused_computation.13 | loop fusion | flops 20971520 | bytes 12648960 | tf_op jit(solution)/shard_map/convert_element_type | solution.py:75
  64.9 1.4 convolution_bitcast_fusion.4
  66.3 0.8 slice-done.1
  67.1 7.6 %fusion.2 = bf16[128,16384]{0,1:T(8,128)(2,1)S(1)} fusion(bf16[128,16384]{0,1:T(8,128)(2,1)S(1)} %fusion.4, bf16[128,128]{1,0:T(8,128)(2,1)S(1)} %copy-done, f32[128,16384]{0,1:T(8,128)S(1)} %bitcast.178, f32[16384]{0:T(1024)S(1)} %get-tuple-element.18, f32[128]{0:T(128)S(1)} %convert_element_type.84), kind=kOutput, calls=%fused_computation.5 | convolution fusion | flops 559939584 | bytes 16876032 | tf_op jit(solution)/shard_map/dot_general | solution.py:53
  74.7 3.5 fusion.21
  78.1 2.5 multiply_reduce_fusion.2
  80.6 2.5 copy.55
  83.1 1.3 fusion.41
  84.5 0.8 copy-done.4
  85.3 0.7 convolution_bitcast_fusion.5
  86.1 9.2 %fusion.8 = f32[64,240]{1,0:T(8,128)S(1)} fusion(bf16[1,240,16384]{2,1,0:T(8,128)(2,1)} %param.10, f32[64,128,128]{2,0,1:T(8,128)} %bitcast.157, f32[64]{0:T(128)S(1)} %get-tuple-element.14, f32[64]{0:T(128)S(1)} %get-tuple-element.16, f32[64]{0:T(128)S(1)} %get-tuple-element.15), kind=kOutput, calls=%fused_computation.21 | convolution fusion | flops 509607936 | bytes 12120832 | tf_op jit(solution)/shard_map/dot_general | solution.py:47
  95.3 0.1 reshape.182
  95.5 0.8 concatenate.3
  96.3 247.7 %all-reduce.4.cloned.1.call-done = f32[40256]{0:T(1024)} async-done(((f32[40256]{0:T(1024)}), f32[40256]{0:T(1024)}) %all-reduce.4.cloned.1.call-update) | async-done | bytes 161040 | tf_op jit(solution)/shard_map/psum | solution.py:189
  344.0 1.6 copy.57
  (61 shorter events, 1.3 us)
Async XLA Ops:
  7.2 12.7 %copy-start = (bf16[128,128]{1,0:T(8,128)(2,1)S(1)}, bf16[128,128]{1,0:T(8,128)(2,1)}, u32[]{:S(2)}) copy-start(bf16[128,128]{1,0:T(8,128)(2,1)} %param.18) | copy-start | bytes 98308
  7.2 336.8 %all-reduce.4.cloned.1.call-start = ((), (), s32[]{:S(2)}) async-start(), calls=%async_computation | async-start | bytes 327680 | tf_op jit(solution)/shard_map/psum | solution.py:189
  12.8 7.1 %copy-start.1 = (f32[64,128,128]{2,0,1:T(8,128)}, f32[64,128,128]{2,0,1:T(8,128)S(1)}, u32[]{:S(2)}) copy-start(f32[64,128,128]{2,0,1:T(8,128)S(1)} %fusion.5) | copy-start | bytes 12582916
  12.8 2.4 copy-start.12
  19.8 4.6 %copy-start.5 = (bf16[128,16384]{0,1:T(8,128)(2,1)}, bf16[128,16384]{0,1:T(8,128)(2,1)S(1)}, u32[]{:S(2)}) copy-start(bf16[128,16384]{0,1:T(8,128)(2,1)S(1)} %get-tuple-element.37) | copy-start | bytes 12582916
  19.8 6.6 %copy-start.8 = (bf16[128]{0:T(256)(128)(2,1)S(1)}, bf16[128]{0:T(256)(128)(2,1)}, u32[]{:S(2)}) copy-start(bf16[128]{0:T(256)(128)(2,1)} %param.19) | copy-start | bytes 772
  24.5 2.0 copy-start.3
  24.5 3.3 copy-start.11
  24.5 3.4 copy-start.7
  24.5 3.5 copy-start.10
  24.5 21.7 %copy-start.9 = (s32[1,12]{1,0:T(1,128)S(1)}, s32[1,12]{1,0:T(1,128)}, u32[]{:S(2)}) copy-start(s32[1,12]{1,0:T(1,128)} %param.14) | copy-start | bytes 148
  28.5 7.6 %collective-permute-start.3 = (f32[4]{0:T(128)S(1)}, f32[4]{0:T(128)S(1)}, u32[]{:S(2)}, u32[]{:S(2)}) collective-permute-start(f32[4]{0:T(128)S(1)} %get-tuple-element.26), channel_id=1, source_target_pairs={{0,1},{1,2},{2,3},{3,4},{4,5},{5,6},{6,7},{7,8},{8,9},{9,10},{10,1... | collective-permute-start | bytes 56 | tf_op jit(solution)/shard_map/ppermute | solution.py:12
  31.2 7.0 %collective-permute-start.4 = (f32[4]{0:T(128)S(1)}, f32[4]{0:T(128)S(1)}, u32[]{:S(2)}, u32[]{:S(2)}) collective-permute-start(f32[4]{0:T(128)S(1)} %get-tuple-element.25), channel_id=1, source_target_pairs={{0,2},{1,3},{2,4},{3,5},{4,6},{5,7},{6,8},{7,9},{8,10},{9,11},{10,... | collective-permute-start | bytes 56 | tf_op jit(solution)/shard_map/ppermute | solution.py:12
  32.5 6.3 %collective-permute-start.5 = (f32[4]{0:T(128)S(1)}, f32[4]{0:T(128)S(1)}, u32[]{:S(2)}, u32[]{:S(2)}) collective-permute-start(f32[4]{0:T(128)S(1)} %get-tuple-element.24), channel_id=1, source_target_pairs={{0,3},{1,4},{2,5},{3,6},{4,7},{5,8},{6,9},{7,10},{8,11},{9,12},{10... | collective-permute-start | bytes 56 | tf_op jit(solution)/shard_map/ppermute | solution.py:12
  34.3 5.4 %collective-permute-start = (f32[4]{0:T(128)S(1)}, f32[4]{0:T(128)S(1)}, u32[]{:S(2)}, u32[]{:S(2)}) collective-permute-start(f32[4]{0:T(128)S(1)} %get-tuple-element.30), channel_id=1, source_target_pairs={{0,1},{1,2},{2,3},{3,4},{4,5},{5,6},{6,7},{7,8},{8,9},{9,10},{10,1... | collective-permute-start | bytes 56 | tf_op jit(solution)/shard_map/ppermute | solution.py:12
  34.7 7.1 %collective-permute-start.1 = (f32[4]{0:T(128)S(1)}, f32[4]{0:T(128)S(1)}, u32[]{:S(2)}, u32[]{:S(2)}) collective-permute-start(f32[4]{0:T(128)S(1)} %get-tuple-element.29), channel_id=1, source_target_pairs={{0,2},{1,3},{2,4},{3,5},{4,6},{5,7},{6,8},{7,9},{8,10},{9,11},{10,... | collective-permute-start | bytes 56 | tf_op jit(solution)/shard_map/ppermute | solution.py:12
  36.1 6.3 %collective-permute-start.2 = (f32[4]{0:T(128)S(1)}, f32[4]{0:T(128)S(1)}, u32[]{:S(2)}, u32[]{:S(2)}) collective-permute-start(f32[4]{0:T(128)S(1)} %get-tuple-element.28), channel_id=1, source_target_pairs={{0,3},{1,4},{2,5},{3,6},{4,7},{5,8},{6,9},{7,10},{8,11},{9,12},{10... | collective-permute-start | bytes 56 | tf_op jit(solution)/shard_map/ppermute | solution.py:12
  38.3 4.3 %collective-permute-start.6 = (f32[4]{0:T(128)S(1)}, f32[4]{0:T(128)S(1)}, u32[]{:S(2)}, u32[]{:S(2)}) collective-permute-start(f32[4]{0:T(128)S(1)} %get-tuple-element.34), channel_id=1, source_target_pairs={{0,1},{1,2},{2,3},{3,4},{4,5},{5,6},{6,7},{7,8},{8,9},{9,10},{10,1... | collective-permute-start | bytes 56 | tf_op jit(solution)/shard_map/ppermute | solution.py:12
  38.8 5.7 %collective-permute-start.7 = (f32[4]{0:T(128)S(1)}, f32[4]{0:T(128)S(1)}, u32[]{:S(2)}, u32[]{:S(2)}) collective-permute-start(f32[4]{0:T(128)S(1)} %get-tuple-element.33), channel_id=1, source_target_pairs={{0,2},{1,3},{2,4},{3,5},{4,6},{5,7},{6,8},{7,9},{8,10},{9,11},{10,... | collective-permute-start | bytes 56 | tf_op jit(solution)/shard_map/ppermute | solution.py:12
  39.7 6.3 %collective-permute-start.8 = (f32[4]{0:T(128)S(1)}, f32[4]{0:T(128)S(1)}, u32[]{:S(2)}, u32[]{:S(2)}) collective-permute-start(f32[4]{0:T(128)S(1)} %get-tuple-element.32), channel_id=1, source_target_pairs={{0,3},{1,4},{2,5},{3,6},{4,7},{5,8},{6,9},{7,10},{8,11},{9,12},{10... | collective-permute-start | bytes 56 | tf_op jit(solution)/shard_map/ppermute | solution.py:12
  47.0 3.2 collective-permute-start.9
  47.9 2.7 collective-permute-start.10
  49.9 4.5 %collective-permute-start.11 = (f32[4]{0:T(128)S(1)}, f32[4]{0:T(128)S(1)}, u32[]{:S(2)}, u32[]{:S(2)}) collective-permute-start(f32[4]{0:T(128)S(1)} %get-tuple-element.20), channel_id=1, source_target_pairs={{0,29},{1,30},{2,31},{3,0},{4,1},{5,2},{6,3},{7,4},{8,5},{9,6},{10... | collective-permute-start | bytes 56 | tf_op jit(solution)/shard_map/ppermute | solution.py:12
  54.9 10.0 %copy-start.6 = (bf16[128,16384]{0,1:T(8,128)(2,1)S(1)}, bf16[128,16384]{0,1:T(8,128)(2,1)}, u32[]{:S(2)}) copy-start(bf16[128,16384]{0,1:T(8,128)(2,1)} %copy-done.5) | copy-start | bytes 12582916
  54.9 11.4 %slice-start = ((s8[8388608]{0:T(1024)(128)(4,1)}), s8[4194304]{0:T(1024)(128)(4,1)S(1)}, s32[]{:S(2)}) async-start(s8[8388608]{0:T(1024)(128)(4,1)} %bitcast.177), calls=%async_computation.1 | async-start | bytes 8388608
  64.9 2.2 slice-start.1
  67.1 7.6 %copy-start.2 = (f32[64,128,128]{2,0,1:T(8,128)S(1)}, f32[64,128,128]{2,0,1:T(8,128)}, u32[]{:S(2)}) copy-start(f32[64,128,128]{2,0,1:T(8,128)} %copy-done.1) | copy-start | bytes 12582916
  83.1 2.2 copy-start.4
Sparse Core Ops, SparseCore 0:
  96.5 247.5 all-reduce.3
where the time goes:
time: 353 us; the launch traced here: 352 us
  waiting for transfers between devices  256 us (73%)
  matrix products  38.8 us (11%)
  other arithmetic  16.9 us (5%)
  starting transfers between devices  16.2 us (5%)
  between operations  14.3 us (4%)
  local copies, waits for them, and re-layouts  10.2 us (3%)
    psum x1, waiting for transfers between devices, on_device(): weight_grads = lax.psum(local_grads, ('state', 'tile'))  248 us
    ppermute x12, starting transfers between devices, from_behind(): lax.ppermute(value, axis, [(i, (i + by) % peers) for i in range(peers)])  16.2 us
    dot_general x3, matrix products, contract_last(): lax.dot_general(left, right, (((1,), (1,)), ((), ())), preferred_element_...  12 us
    dot_general x2, matrix products, contract_first(): lax.dot_general(left, right, (((0,), (0,)), ((), ())), preferred_element_...  11 us
    convert_element_type x1, other arithmetic, backward(): d_h3 = (d_a3 * silu_parts(h_three)[1]).astype(jnp.bfloat16)  9.98 us
    ppermute x12, waiting for transfers between devices, from_behind(): lax.ppermute(value, axis, [(i, (i + by) % peers) for i in range(peers)])  8.37 us
  transfers between devices with their start and end apart: 13, of which 7 were waited for; matrix products, arithmetic and copies ran while one was open for 0% of the time, Pallas kernels for 0%

commit v1 on v0

--- a/solution.py
+++ b/solution.py
@@ -1,3 +1,4 @@
+import functools
 import jax
 import jax.numpy as jnp
 from jax import lax
@@ -5,6 +6,14 @@
 
 MOST = 4
 REACH = 4
+
+
+def draw_pairs_all_here(t0, axis_name, axis_id):
+    everything = lax.psum(lax.psum(t0, axis_name), axis_id)
+    return everything
+
+
+_extend_thing = functools.partial(draw_pairs_all_here, axis_name="state", axis_id="tile")
 
 
 def from_behind(value, axis, by):
@@ -186,7 +195,7 @@
     slot_adjoint = jnp.sum(select * returned[None, :], axis=1)
     cotangent = pixel_cotangent(member, slot_adjoint, row_len)
     local_grads = backward(pixels, saved, taps, w_second, w_third, w_head, cotangent, row_len)
-    weight_grads = lax.psum(local_grads, ("state", "tile"))
+    weight_grads = _extend_thing(local_grads)
     return (county_mean[None, :], weight_grads)
 
 

time: 353 us -> 289 us (0.82)
  waiting for transfers between devices: 256 us -> 192 us
    psum x1 -> x2, waiting for transfers between devices: 248 us -> 184 us  [draw_pairs_all_here(): everything = lax.psum(lax.psum(t0, axis_name), axis_id)]
  transfers between devices with their start and end apart: 13 -> 14, of which waited for: 7 -> 8; matrix products, arithmetic and copies ran while one was open for 0% -> 0% of each run, Pallas kernels for 0% -> 0%
where the time goes in v1:
time: 289 us; the launch traced here: 288 us
  waiting for transfers between devices  192 us (66%)
  matrix products  38.8 us (13%)
  other arithmetic  16.9 us (6%)
  starting transfers between devices  16.3 us (6%)
  between operations  14.3 us (5%)
  local copies, waits for them, and re-layouts  10.2 us (4%)
    psum x2, waiting for transfers between devices, draw_pairs_all_here(): everything = lax.psum(lax.psum(t0, axis_name), axis_id)  184 us
    ppermute x12, starting transfers between devices, from_behind(): lax.ppermute(value, axis, [(i, (i + by) % peers) for i in range(peers)])  16.2 us
    dot_general x3, matrix products, contract_last(): lax.dot_general(left, right, (((1,), (1,)), ((), ())), preferred_element_...  12 us
    dot_general x2, matrix products, contract_first(): lax.dot_general(left, right, (((0,), (0,)), ((), ())), preferred_element_...  11 us
    convert_element_type x1, other arithmetic, backward(): d_h3 = (d_a3 * silu_parts(h_three)[1]).astype(jnp.bfloat16)  9.98 us
    ppermute x12, waiting for transfers between devices, from_behind(): lax.ppermute(value, axis, [(i, (i + by) % peers) for i in range(peers)])  8.37 us
  transfers between devices with their start and end apart: 14, of which 8 were waited for; matrix products, arithmetic and copies ran while one was open for 0% of the time, Pallas kernels for 0%

profile of v1, /device:TPU:1, one launch (start us, length us, event | category | flops | bytes accessed | tf_op | source)
XLA Modules:
  0.0 288.4 jit_solution(13477728835380295256)
XLA Ops:
  7.2 0.8 slice_bitcast_fusion.5
  8.0 4.7 %fusion.5 = f32[64,128,128]{2,0,1:T(8,128)S(1)} fusion(bf16[64,240]{1,0:T(8,128)(2,1)} %param.15, bf16[1,240,16384]{2,1,0:T(8,128)(2,1)} %param.10), kind=kOutput, calls=%fused_computation.18 | convolution fusion | flops 503316480 | bytes 12089344 | tf_op jit(solution)/shard_map/dot_general | solution.py:68
  12.8 2.4 fusion.18
  15.2 4.6 %multiply_convert_fusion = (bf16[128,16384]{0,1:T(8,128)(2,1)S(1)}, f32[128,16384]{0,1:T(8,128)}) fusion(bf16[64,16384]{1,0:T(8,128)(2,1)S(1)} %fusion.18, bf16[128,64]{0,1:T(8,128)(2,1)S(1)} %copy-done.12), kind=kOutput, calls=%fused_computation.16 | convolution fusion | flops 278921216 | bytes 14696448 | tf_op jit(solution)/shard_map/dot_general | solution.py:71
  19.8 4.6 %add_convert_fusion = (bf16[128,16384]{0,1:T(8,128)(2,1)S(1)}, f32[128,16384]{0,1:T(8,128)}) fusion(bf16[128,16384]{0,1:T(8,128)(2,1)S(1)} %get-tuple-element.37, bf16[128,128]{1,0:T(8,128)(2,1)S(1)} %copy-done), kind=kOutput, calls=%fused_computation.14 | convolution fusion | flops 551550976 | bytes 16809984 | tf_op jit(solution)/shard_map/dot_general | solution.py:73
  24.5 1.9 copy-done.3
  26.5 1.2 fusion.38
  27.6 0.1 reduce_sum.147
  27.8 0.1 convert_reduce_fusion
  28.0 0.2 select_reduce_fusion
  28.2 0.2 convert_reduce_fusion.1
  28.5 2.7 collective-permute-start.3
  31.2 1.3 collective-permute-start.4
  32.5 1.7 collective-permute-start.5
  34.3 0.5 collective-permute-start
  34.7 1.3 collective-permute-start.1
  36.1 2.1 collective-permute-start.2
  38.3 0.5 collective-permute-start.6
  38.7 0.1 collective-permute-done.5
  38.8 0.8 collective-permute-start.7
  39.7 2.2 collective-permute-start.8
  41.9 0.6 collective-permute-done.2
  42.6 2.0 collective-permute-done.7
  44.6 1.5 collective-permute-done.8
  46.2 0.5 fusion.40
  46.8 0.2 fusion.28
  47.0 0.9 collective-permute-start.9
  47.9 2.0 collective-permute-start.10
  49.9 0.3 collective-permute-start.11
  50.2 0.4 collective-permute-done.10
  50.6 3.8 %collective-permute-done.11 = f32[4]{0:T(128)S(1)} collective-permute-done((f32[4]{0:T(128)S(1)}, f32[4]{0:T(128)S(1)}, u32[]{:S(2)}, u32[]{:S(2)}) %collective-permute-start.11) | collective-permute-done | bytes 48 | tf_op jit(solution)/shard_map/ppermute | solution.py:21
  54.5 0.2 select_reduce_fusion.2
  54.9 10.0 %fusion.4 = bf16[128,16384]{0,1:T(8,128)(2,1)S(1)} fusion(f32[128,16384]{0,1:T(8,128)} %get-tuple-element.40, f32[16384]{0:T(1024)S(1)} %get-tuple-element.18, f32[128]{0:T(128)S(1)} %convert_element_type.84), kind=kLoop, calls=%fused_computation.13 | loop fusion | flops 20971520 | bytes 12648960 | tf_op jit(solution)/shard_map/convert_element_type | solution.py:84
  64.9 1.4 convolution_bitcast_fusion.4
  66.3 0.8 slice-done.1
  67.1 7.6 %fusion.2 = bf16[128,16384]{0,1:T(8,128)(2,1)S(1)} fusion(bf16[128,16384]{0,1:T(8,128)(2,1)S(1)} %fusion.4, bf16[128,128]{1,0:T(8,128)(2,1)S(1)} %copy-done, f32[128,16384]{0,1:T(8,128)S(1)} %bitcast.178, f32[16384]{0:T(1024)S(1)} %get-tuple-element.18, f32[128]{0:T(128)S(1)} %convert_element_type.84), kind=kOutput, calls=%fused_computation.5 | convolution fusion | flops 559939584 | bytes 16876032 | tf_op jit(solution)/shard_map/dot_general | solution.py:62
  74.7 3.5 %fusion.21 = f32[8,128,8,128]{3,2,1,0:T(8,128)S(1)} fusion(bf16[128,16384]{0,1:T(8,128)(2,1)S(1)} %fusion.2, bf16[128,64]{0,1:T(8,128)(2,1)S(1)} %copy-done.12, f32[64,128,128]{2,0,1:T(8,128)S(1)} %copy-done.2, f32[64]{0:T(128)S(1)} %get-tuple-element.15, f32[64]{0:T(128)S(1)} %get-tuple-element.16, f32[64]{0:T(128)S(1)} %get-tuple-element.14), kind=kOutput, calls=%fused_computation.43 | convolution fusion | flops 282066944 | bytes 12600064 | tf_op jit(solution)/shard_map/dot_general | solution.py:62
  78.1 2.5 multiply_reduce_fusion.2
  80.6 2.5 copy.55
  83.1 1.3 fusion.41
  84.5 0.8 copy-done.4
  85.3 0.7 convolution_bitcast_fusion.5
  86.1 9.2 %fusion.8 = f32[64,240]{1,0:T(8,128)S(1)} fusion(bf16[1,240,16384]{2,1,0:T(8,128)(2,1)} %param.10, f32[64,128,128]{2,0,1:T(8,128)} %bitcast.157, f32[64]{0:T(128)S(1)} %get-tuple-element.14, f32[64]{0:T(128)S(1)} %get-tuple-element.16, f32[64]{0:T(128)S(1)} %get-tuple-element.15), kind=kOutput, calls=%fused_computation.21 | convolution fusion | flops 509607936 | bytes 12120832 | tf_op jit(solution)/shard_map/dot_general | solution.py:56
  95.3 0.1 reshape.182
  95.5 0.8 concatenate.3
  96.4 67.1 %all-reduce.5.cloned.1.call-done = f32[40256]{0:T(1024)} async-done(((f32[40256]{0:T(1024)}), f32[40256]{0:T(1024)}) %all-reduce.5.cloned.1.call-update) | async-done | bytes 161040 | tf_op jit(solution)/shard_map/psum | solution.py:12
  163.5 116.5 %all-reduce.7.cloned.1.call-done = f32[40256]{0:T(1024)} async-done(((f32[40256]{0:T(1024)}), f32[40256]{0:T(1024)}) %all-reduce.7.cloned.1.call-update) | async-done | bytes 161040 | tf_op jit(solution)/shard_map/psum | solution.py:12
  280.0 1.6 copy.58
  (64 shorter events, 1.5 us)
Async XLA Ops:
  7.2 12.7 %copy-start = (bf16[128,128]{1,0:T(8,128)(2,1)S(1)}, bf16[128,128]{1,0:T(8,128)(2,1)}, u32[]{:S(2)}) copy-start(bf16[128,128]{1,0:T(8,128)(2,1)} %param.18) | copy-start | bytes 98308
  7.2 156.3 %all-reduce.5.cloned.1.call-start = ((), (), s32[]{:S(2)}) async-start(), calls=%async_computation | async-start | bytes 327680 | tf_op jit(solution)/shard_map/psum | solution.py:12
  12.8 7.1 %copy-start.1 = (f32[64,128,128]{2,0,1:T(8,128)}, f32[64,128,128]{2,0,1:T(8,128)S(1)}, u32[]{:S(2)}) copy-start(f32[64,128,128]{2,0,1:T(8,128)S(1)} %fusion.5) | copy-start | bytes 12582916
  12.8 2.4 copy-start.12
  19.8 4.6 %copy-start.5 = (bf16[128,16384]{0,1:T(8,128)(2,1)}, bf16[128,16384]{0,1:T(8,128)(2,1)S(1)}, u32[]{:S(2)}) copy-start(bf16[128,16384]{0,1:T(8,128)(2,1)S(1)} %get-tuple-element.37) | copy-start | bytes 12582916
  19.8 6.6 %copy-start.8 = (bf16[128]{0:T(256)(128)(2,1)S(1)}, bf16[128]{0:T(256)(128)(2,1)}, u32[]{:S(2)}) copy-start(bf16[128]{0:T(256)(128)(2,1)} %param.19) | copy-start | bytes 772
  24.5 2.0 copy-start.3
  24.5 3.3 %copy-start.11 = (s32[1,128]{1,0:T(1,128)S(1)}, s32[1,128]{1,0:T(1,128)}, u32[]{:S(2)}) copy-start(s32[1,128]{1,0:T(1,128)} %param.11) | copy-start | bytes 1540
  24.5 3.4 %copy-start.7 = (s32[1,384]{1,0:T(1,128)S(1)}, s32[1,384]{1,0:T(1,128)}, u32[]{:S(2)}) copy-start(s32[1,384]{1,0:T(1,128)} %param.13) | copy-start | bytes 4612
  24.5 3.5 %copy-start.10 = (s32[1,8]{1,0:T(1,128)S(1)}, s32[1,8]{1,0:T(1,128)}, u32[]{:S(2)}) copy-start(s32[1,8]{1,0:T(1,128)} %param.12) | copy-start | bytes 100
  24.5 21.7 %copy-start.9 = (s32[1,12]{1,0:T(1,128)S(1)}, s32[1,12]{1,0:T(1,128)}, u32[]{:S(2)}) copy-start(s32[1,12]{1,0:T(1,128)} %param.14) | copy-start | bytes 148
  28.5 7.6 %collective-permute-start.3 = (f32[4]{0:T(128)S(1)}, f32[4]{0:T(128)S(1)}, u32[]{:S(2)}, u32[]{:S(2)}) collective-permute-start(f32[4]{0:T(128)S(1)} %get-tuple-element.26), channel_id=1, source_target_pairs={{0,1},{1,2},{2,3},{3,4},{4,5},{5,6},{6,7},{7,8},{8,9},{9,10},{10,1... | collective-permute-start | bytes 56 | tf_op jit(solution)/shard_map/ppermute | solution.py:21
  31.2 7.0 %collective-permute-start.4 = (f32[4]{0:T(128)S(1)}, f32[4]{0:T(128)S(1)}, u32[]{:S(2)}, u32[]{:S(2)}) collective-permute-start(f32[4]{0:T(128)S(1)} %get-tuple-element.25), channel_id=1, source_target_pairs={{0,2},{1,3},{2,4},{3,5},{4,6},{5,7},{6,8},{7,9},{8,10},{9,11},{10,... | collective-permute-start | bytes 56 | tf_op jit(solution)/shard_map/ppermute | solution.py:21
  32.5 6.3 %collective-permute-start.5 = (f32[4]{0:T(128)S(1)}, f32[4]{0:T(128)S(1)}, u32[]{:S(2)}, u32[]{:S(2)}) collective-permute-start(f32[4]{0:T(128)S(1)} %get-tuple-element.24), channel_id=1, source_target_pairs={{0,3},{1,4},{2,5},{3,6},{4,7},{5,8},{6,9},{7,10},{8,11},{9,12},{10... | collective-permute-start | bytes 56 | tf_op jit(solution)/shard_map/ppermute | solution.py:21
  34.3 5.4 %collective-permute-start = (f32[4]{0:T(128)S(1)}, f32[4]{0:T(128)S(1)}, u32[]{:S(2)}, u32[]{:S(2)}) collective-permute-start(f32[4]{0:T(128)S(1)} %get-tuple-element.30), channel_id=1, source_target_pairs={{0,1},{1,2},{2,3},{3,4},{4,5},{5,6},{6,7},{7,8},{8,9},{9,10},{10,1... | collective-permute-start | bytes 56 | tf_op jit(solution)/shard_map/ppermute | solution.py:21
  34.7 7.1 %collective-permute-start.1 = (f32[4]{0:T(128)S(1)}, f32[4]{0:T(128)S(1)}, u32[]{:S(2)}, u32[]{:S(2)}) collective-permute-start(f32[4]{0:T(128)S(1)} %get-tuple-element.29), channel_id=1, source_target_pairs={{0,2},{1,3},{2,4},{3,5},{4,6},{5,7},{6,8},{7,9},{8,10},{9,11},{10,... | collective-permute-start | bytes 56 | tf_op jit(solution)/shard_map/ppermute | solution.py:21
  36.1 6.3 %collective-permute-start.2 = (f32[4]{0:T(128)S(1)}, f32[4]{0:T(128)S(1)}, u32[]{:S(2)}, u32[]{:S(2)}) collective-permute-start(f32[4]{0:T(128)S(1)} %get-tuple-element.28), channel_id=1, source_target_pairs={{0,3},{1,4},{2,5},{3,6},{4,7},{5,8},{6,9},{7,10},{8,11},{9,12},{10... | collective-permute-start | bytes 56 | tf_op jit(solution)/shard_map/ppermute | solution.py:21
  38.3 4.3 %collective-permute-start.6 = (f32[4]{0:T(128)S(1)}, f32[4]{0:T(128)S(1)}, u32[]{:S(2)}, u32[]{:S(2)}) collective-permute-start(f32[4]{0:T(128)S(1)} %get-tuple-element.34), channel_id=1, source_target_pairs={{0,1},{1,2},{2,3},{3,4},{4,5},{5,6},{6,7},{7,8},{8,9},{9,10},{10,1... | collective-permute-start | bytes 56 | tf_op jit(solution)/shard_map/ppermute | solution.py:21
  38.8 5.7 %collective-permute-start.7 = (f32[4]{0:T(128)S(1)}, f32[4]{0:T(128)S(1)}, u32[]{:S(2)}, u32[]{:S(2)}) collective-permute-start(f32[4]{0:T(128)S(1)} %get-tuple-element.33), channel_id=1, source_target_pairs={{0,2},{1,3},{2,4},{3,5},{4,6},{5,7},{6,8},{7,9},{8,10},{9,11},{10,... | collective-permute-start | bytes 56 | tf_op jit(solution)/shard_map/ppermute | solution.py:21
  39.7 6.3 %collective-permute-start.8 = (f32[4]{0:T(128)S(1)}, f32[4]{0:T(128)S(1)}, u32[]{:S(2)}, u32[]{:S(2)}) collective-permute-start(f32[4]{0:T(128)S(1)} %get-tuple-element.32), channel_id=1, source_target_pairs={{0,3},{1,4},{2,5},{3,6},{4,7},{5,8},{6,9},{7,10},{8,11},{9,12},{10... | collective-permute-start | bytes 56 | tf_op jit(solution)/shard_map/ppermute | solution.py:21
  47.0 3.2 %collective-permute-start.9 = (f32[4]{0:T(128)S(1)}, f32[4]{0:T(128)S(1)}, u32[]{:S(2)}, u32[]{:S(2)}) collective-permute-start(f32[4]{0:T(128)S(1)} %get-tuple-element.22), channel_id=1, source_target_pairs={{0,31},{1,0},{2,1},{3,2},{4,3},{5,4},{6,5},{7,6},{8,7},{9,8},{10,9... | collective-permute-start | bytes 56 | tf_op jit(solution)/shard_map/ppermute | solution.py:21
  47.9 2.7 collective-permute-start.10
  49.9 4.5 %collective-permute-start.11 = (f32[4]{0:T(128)S(1)}, f32[4]{0:T(128)S(1)}, u32[]{:S(2)}, u32[]{:S(2)}) collective-permute-start(f32[4]{0:T(128)S(1)} %get-tuple-element.20), channel_id=1, source_target_pairs={{0,29},{1,30},{2,31},{3,0},{4,1},{5,2},{6,3},{7,4},{8,5},{9,6},{10... | collective-permute-start | bytes 56 | tf_op jit(solution)/shard_map/ppermute | solution.py:21
  54.9 10.0 %copy-start.6 = (bf16[128,16384]{0,1:T(8,128)(2,1)S(1)}, bf16[128,16384]{0,1:T(8,128)(2,1)}, u32[]{:S(2)}) copy-start(bf16[128,16384]{0,1:T(8,128)(2,1)} %copy-done.5) | copy-start | bytes 12582916
  54.9 11.4 %slice-start = ((s8[8388608]{0:T(1024)(128)(4,1)}), s8[4194304]{0:T(1024)(128)(4,1)S(1)}, s32[]{:S(2)}) async-start(s8[8388608]{0:T(1024)(128)(4,1)} %bitcast.177), calls=%async_computation.2 | async-start | bytes 8388608
  64.9 2.2 slice-start.1
  67.1 7.6 %copy-start.2 = (f32[64,128,128]{2,0,1:T(8,128)S(1)}, f32[64,128,128]{2,0,1:T(8,128)}, u32[]{:S(2)}) copy-start(f32[64,128,128]{2,0,1:T(8,128)} %copy-done.1) | copy-start | bytes 12582916
  83.1 2.2 copy-start.4
  96.3 183.7 %all-reduce.7.cloned.1.call-start = ((), (), s32[]{:S(2)}) async-start(), calls=%async_computation.1 | async-start | bytes 327680 | tf_op jit(solution)/shard_map/psum | solution.py:12
Sparse Core Ops, SparseCore 0:
  96.5 67.0 all-reduce.4
  166.8 113.1 all-reduce.6
